TPU v7x, 256 devices: a whole 4x4x8 slice. The times are simulated.
256 devices in a mesh: expert: 8 (over x, core), latent: 32 (over y, z).
Axes of the slice: x: 4, y: 4, z: 8, core: 2. Of those that a mesh axis runs over, the one named last changes fastest.
Arguments:
- tokens: bfloat16 [2048, 2560], P(('expert', 'latent')), may hold values from -6 to 6
- route: int32 [2048, 1], P(('expert', 'latent')), may hold values from 0 to 7; in each aligned block of 8 rows (0 to 7, 8 to 15, ...) at most 2 rows name the same one
- blocks: int32 [2048, 64], P(('expert', 'latent')), may hold values from 0 to 255, all different within a row
- weight: bfloat16 [8, 2560, 32768], P('expert', None, 'latent'), may hold values from -0.125 to 0.125
- enc_bias: float32 [8, 32768], P('expert', 'latent'), may hold values from -3 to 3
- dec_bias: float32 [2560], replicated, may hold values from -3 to 3
Outputs:
- grad_weight: bfloat16 [8, 2560, 32768], P('expert', None, 'latent')
- grad_enc: float32 [8, 32768], P('expert', 'latent')
- grad_dec: float32 [2560], replicated
- loss: float32 [], replicated
Inputs may be any that keep to these rules, and one draw needn't show every extreme that they name: `route`: within the rows of one device (aligned blocks of 8 rows) no expert is named by more than 2 rows. Each row lists 64 different blocks.
All inputs are finite; a program needn't handle non-finite values.
Results may differ from a plain program's by a relative error of at most 0.012.
The roundings to bfloat16 on the way count: a program that leaves them out, or rounds other values in their place, can miss the bound.
Values may be sent and summed in bfloat16 or wider, within the bound.
No kernel may reach another device: no remote copies, remote signals or barrier semaphores. Data moves between devices by JAX's collectives and lax.ppermute only.
A program may use at most 128 MiB of HBM per device.

v0:
```python
import jax
import jax.numpy as jnp
from jax import lax
from jax.sharding import PartitionSpec as P

BLK = 128
CAP = 2


def shards(tokens, route, blocks, weight, enc_bias, dec_bias):
    n_expert = lax.axis_size("expert")
    n_latent = lax.axis_size("latent")
    width = tokens.shape[1]
    list_len = blocks.shape[1]
    expert_of = route[:, 0]
    one_hot = (expert_of[:, None] == jnp.arange(n_expert, dtype=jnp.int32)[None, :]).astype(
        jnp.int32
    )
    earlier = jnp.sum((jnp.cumsum(one_hot, axis=0) - one_hot) * one_hot, axis=1)
    target = expert_of * CAP + earlier
    send_rows = jnp.zeros((n_expert * CAP, width), jnp.bfloat16).at[target].set(tokens)
    send_rows = send_rows.reshape(n_expert, CAP, width)
    send_lists = jnp.full((n_expert * CAP, list_len), -1, jnp.int32).at[target].set(blocks)
    send_lists = send_lists.reshape(n_expert, CAP, list_len)
    got_rows, got_lists = (
        lax.all_to_all(send_rows, "expert", split_axis=0, concat_axis=0, tiled=True),
        lax.all_to_all(send_lists, "expert", split_axis=0, concat_axis=0, tiled=True),
    )
    all_rows, all_lists = (
        lax.all_gather(got_rows[None], "latent", axis=0, tiled=True),
        lax.all_gather(got_lists[None], "latent", axis=0, tiled=True),
    )
    token_rows = all_rows.reshape(-1, width)
    listed = all_lists.reshape(-1, list_len)
    row_count = token_rows.shape[0]
    valid = (listed[:, 0] >= 0).astype(jnp.float32)
    slice_index = lax.axis_index("latent")
    weights_here = weight[0]
    per_slice = weights_here.shape[1] // BLK
    own_blocks = slice_index * per_slice + jnp.arange(per_slice, dtype=jnp.int32)
    chosen = jnp.any(listed[:, :, None] == own_blocks[None, None, :], axis=1).astype(jnp.float32)
    mask = jnp.repeat(chosen, BLK, axis=1)
    rows_f32 = token_rows.astype(jnp.float32)
    shifted = (rows_f32 - dec_bias).astype(jnp.bfloat16)
    pre_act = jnp.dot(shifted, weights_here, preferred_element_type=jnp.float32) + enc_bias[0]
    active = jnp.maximum(pre_act, 0.0) * mask
    active_bf = active.astype(jnp.bfloat16)
    share = row_count // n_latent
    first_row = slice_index * share
    along_width = (((1,), (1,)), ((), ()))
    partial_sum = lax.dot_general(
        active_bf, weights_here, along_width, preferred_element_type=jnp.float32
    )
    summed = lax.psum(partial_sum, "latent")
    error_all = (summed + dec_bias - rows_f32) * valid[:, None]
    error_bf = error_all.astype(jnp.bfloat16)
    error_share = lax.dynamic_slice_in_dim(error_all, first_row, share, 0)
    grad_act = jnp.dot(error_bf, weights_here, preferred_element_type=jnp.float32)
    grad_pre = grad_act * (pre_act > 0.0).astype(jnp.float32) * mask
    grad_pre_bf = grad_pre.astype(jnp.bfloat16)
    along_rows = (((0,), (0,)), ((), ()))
    grad_here = lax.dot_general(
        shifted, grad_pre_bf, along_rows, preferred_element_type=jnp.float32
    )
    grad_here = grad_here + lax.dot_general(
        error_bf, active_bf, along_rows, preferred_element_type=jnp.float32
    )
    grad_bias = jnp.sum(grad_pre, axis=0)
    pulled = jnp.dot(
        weights_here, grad_bias.astype(jnp.bfloat16), preferred_element_type=jnp.float32
    )
    bias_term = jnp.sum(error_share, axis=0) - pulled
    loss_term = 0.5 * jnp.sum(error_share * error_share)
    grad_dec, loss_sum = lax.psum((bias_term, loss_term), ("expert", "latent"))
    loss = loss_sum / (tokens.shape[0] * n_expert * n_latent)
    return (grad_here.astype(jnp.bfloat16)[None], grad_bias[None], grad_dec, loss)


def solution(mesh):
    return jax.shard_map(
        shards,
        mesh=mesh,
        in_specs=(
            P(("expert", "latent"), None),
            P(("expert", "latent"), None),
            P(("expert", "latent"), None),
            P("expert", None, "latent"),
            P("expert", "latent"),
            P(),
        ),
        out_specs=(P("expert", None, "latent"), P("expert", "latent"), P(), P()),
        check_vma=False,
    )
```

profile of v0, /device:TPU:1, one launch (start us, length us, event | category | flops | bytes accessed | tf_op | source)
XLA Modules:
  0.0 402.3 jit_solution(3232776257881222928)
XLA Ops:
  7.2 0.0 all-gather.4.cloned.1.call-start
  7.2 0.7 fusion.24
  8.0 0.8 select_reduce_fusion
  8.8 0.7 fusion.25
  9.5 0.9 scatter_custom_fusion
  10.4 11.2 %all_to_all.10 = bf16[8,2,2560]{2,1,0:T(2,128)(2,1)} all-to-all(bf16[8,2,2560]{2,1,0:T(2,128)(2,1)S(1)} %reshape.33), channel_id=1, replica_groups=mesh['expert'=8,'latent'=32] {'expert'}, dimensions={0} | all-to-all | bytes 163840 | tf_op jit(solution)/shard_map/all_to_all | solution.py:26
  21.6 0.0 all-gather.4.cloned.1.call-update
  21.7 0.8 scatter_custom_fusion.1
  22.4 0.7 reshape.68
  23.1 4.0 all-to-all-start.1
  27.1 4.5 %all-to-all-done.1 = s32[8,1,128]{2,1,0:T(1,128)S(1)} async-done(((s32[8,1,128]{2,1,0:T(1,128)}), s32[8,1,128]{2,1,0:T(1,128)S(1)}, u32[]{:S(2)}, u32[]{:S(2)}) %all-to-all-start.1) | async-done | bytes 4128 | tf_op jit(solution)/shard_map/all_to_all | solution.py:27
  31.6 0.5 broadcast.43
  32.2 0.7 reduce.4
  32.8 0.1 reshape.69
  32.9 40.8 %all-gather.1 = s32[256,2,64]{2,1,0:T(2,128)S(1)} all-gather(s32[8,2,64]{2,1,0:T(2,128)S(1)} %reshape.69), channel_id=3, replica_groups=mesh['expert'=8,'latent'=32] {'latent'}, dimensions={0}, use_global_device_ids=true | all-gather | bytes 135168 | tf_op jit(solution)/shard_map/all_gather | solution.py:31
  73.7 0.1 copy.12
  73.8 0.2 compare_reduce_fusion
  74.1 0.1 copy.13
  74.2 24.0 %all-gather.4.cloned.1.call-done = bf16[256,2,2560]{2,1,0:T(2,128)(2,1)} async-done(((bf16[8,2,2560]{2,1,0:T(2,128)(2,1)}), bf16[256,2,2560]{2,1,0:T(2,128)(2,1)}) %all-gather.4.cloned.1.call-update) | async-done | bytes 2621456 | tf_op jit(solution)/shard_map/all_gather | solution.py:30
  98.1 3.5 convert_element_type.56
  101.7 2.3 subtract_convert_fusion
  104.0 0.0 copy-start.6
  104.0 2.6 convert_element_type.47
  106.6 0.6 broadcast_in_dim.32
  107.2 0.0 copy-start.1
  107.2 0.0 copy-done.6
  107.2 0.0 slice-start.3
  107.3 8.7 %fusion.11 = (bf16[512,1024]{1,0:T(8,128)(2,1)S(1)}, f32[512,1024]{1,0:T(8,128)}) fusion(f32[64,8,8,128]{3,2,1,0:T(8,128)S(1)} %bitcast.51, f32[1024]{0:T(1024)S(1)} %bitcast.57, bf16[512,2560]{1,0:T(8,128)(2,1)} %convert_element_type.47, bf16[1,2560,1024]{2,1,0:T(8,128)(2,1)} %param.9), kind=kOutput, calls=%fused_computation.19 | convolution fusion | flops 2686451712 | bytes 13111296 | tf_op jit(solution)/shard_map/dot_general | solution.py:45
  116.0 1.0 copy-done.3
  117.0 4.7 %fusion.4 = f32[512,2560]{1,0:T(8,128)} fusion(bf16[512,1024]{1,0:T(8,128)(2,1)S(1)} %get-tuple-element.8, bf16[1,2560,1024]{2,1,0:T(8,128)(2,1)S(1)} %bitcast.46), kind=kOutput, calls=%fused_computation.7 | convolution fusion | flops 2684354560 | bytes 11534336 | tf_op jit(solution)/shard_map/dot_general | solution.py:51
  121.7 0.0 all-reduce.3.cloned.1.call-update
  121.7 0.1 convert_reduce_fusion
  121.8 1.6 copy-done
  123.4 2.9 reshape.36
  126.4 168.2 %all-reduce.3.cloned.1.call-done = f32[512,2560]{1,0:T(8,128)} async-done(((f32[512,2560]{1,0:T(8,128)}), f32[512,2560]{1,0:T(8,128)}) %all-reduce.3.cloned.1.call-update) | async-done | bytes 5242896 | tf_op jit(solution)/shard_map/psum | solution.py:54
  294.5 4.9 %subtract_multiply_fusion = f32[512,2560]{1,0:T(8,128)S(1)} fusion(f32[512,2560]{1,0:T(8,128)} %reshape.36, f32[512,2560]{1,0:T(8,128)} %all-reduce.3.cloned.1.call-done, f32[512]{0:T(512)S(1)} %convert_reduce_fusion, f32[2560]{0:T(1024)S(1)} %copy-done.4), kind=kLoop, calls=%fused_computation.11 | loop fusion | flops 3932160 | bytes 15740928 | tf_op jit(solution)/shard_map/mul | solution.py:55
  299.5 0.0 slice-start.1
  299.5 5.9 %fusion.26 = (f32[1024]{0:T(1024)S(1)}, bf16[512,1024]{1,0:T(8,128)(2,1)S(1)}) fusion(f32[64,8,8,128]{3,2,1,0:T(8,128)S(1)} %bitcast.52, bf16[1,2560,1024]{2,1,0:T(8,128)(2,1)} %param.9, f32[512,2560]{1,0:T(8,128)S(1)} %subtract_multiply_fusion, f32[512,1024]{1,0:T(8,128)S(1)} %copy-done.7, f32[1024]{0:T(1024)S(1)} %bitcast.58), kind=kOutput, calls=%fused_computation.40 | convolution fusion | flops 2688809984 | bytes 15736832 | tf_op jit(solution)/shard_map/dot_general | solution.py:58
  305.4 0.0 copy-start.5
  305.4 0.0 slice-done
  305.4 0.0 slice-done.1
  305.4 0.0 slice-start.4
  305.5 3.0 fusion.9
  308.5 0.0 slice-start.5
  308.5 6.5 %fusion.8 = bf16[1,2560,1024]{2,1,0:T(8,128)(2,1)} fusion(f32[2560,1024]{1,0:T(8,128)S(1)} %fusion.9, bf16[512,1024]{1,0:T(8,128)(2,1)} %copy-done.3, f32[512,2560]{1,0:T(8,128)S(1)} %subtract_multiply_fusion), kind=kOutput, calls=%fused_computation.14 | convolution fusion | flops 2690908160 | bytes 22020096 | tf_op jit(solution)/shard_map/dot_general | solution.py:65
  315.0 0.6 multiply_reduce_fusion
  315.6 1.5 fusion.16
  317.8 75.9 %all-reduce = (f32[2560]{0:T(1024)}, f32[]{:T(128)}) all-reduce(f32[2560]{0:T(1024)S(1)} %sub.28, f32[]{:T(128)S(6)} %mul_shard_map.3), channel_id=1, replica_groups=mesh['expert'=8,'latent'=32] {'expert','latent'}, use_global_device_ids=true, to_apply=%region_8.9 | all-reduce | flops 2561 | bytes 20488 | tf_op jit(solution)/shard_map/psum | solution.py:74
  (27 shorter events, 0.1 us)
Async XLA Ops:
  7.2 94.5 %copy-start.4 = (f32[2560]{0:T(1024)S(1)}, f32[2560]{0:T(1024)}, u32[]{:S(2)}) copy-start(f32[2560]{0:T(1024)} %param.11) | copy-start | bytes 30724
  7.2 91.0 %all-gather.4.cloned.1.call-start = ((), (), s32[]{:S(2)}) async-start(), calls=%async_computation.3 | async-start | bytes 2703360 | tf_op jit(solution)/shard_map/all_gather | solution.py:30
  23.1 8.5 %all-to-all-start.1 = ((s32[8,1,128]{2,1,0:T(1,128)}), s32[8,1,128]{2,1,0:T(1,128)S(1)}, u32[]{:S(2)}, u32[]{:S(2)}) async-start(s32[8,1,128]{2,1,0:T(1,128)} %reshape.68), calls=%async_computation.1 | async-start | bytes 8192 | tf_op jit(solution)/shard_map/all_to_all | solution.py:27
  27.1 267.4 %all-reduce.3.cloned.1.call-start = ((), (), s32[]{:S(2)}) async-start(), calls=%async_computation.2 | async-start | bytes 10485760 | tf_op jit(solution)/shard_map/psum | solution.py:54
  104.0 3.2 copy-start.6
  106.6 10.4 %slice-start.2 = ((s8[5242880]{0:T(1024)(128)(4,1)}), s8[4194304]{0:T(1024)(128)(4,1)S(1)}, s32[]{:S(2)}) async-start(s8[5242880]{0:T(1024)(128)(4,1)} %bitcast.45), calls=%async_computation.6 | async-start | bytes 8388608
  107.2 8.8 %copy-start.1 = (f32[512,8,128]{2,1,0:T(8,128)}, f32[512,8,128]{2,1,0:T(8,128)S(1)}, u32[]{:S(2)}) copy-start(f32[512,8,128]{2,1,0:T(8,128)S(1)} %broadcast_in_dim.32) | copy-start | bytes 6291460
  107.2 9.7 %slice-start.3 = ((s8[5242880]{0:T(1024)(128)(4,1)}), s8[1048576]{0:T(1024)(128)(4,1)S(1)}, s32[]{:S(2)}) async-start(s8[5242880]{0:T(1024)(128)(4,1)} %bitcast.45), calls=%async_computation.7 | async-start | bytes 2097152
  116.0 1.0 copy-start.3
  121.7 1.7 copy-start
  126.3 173.1 %copy-start.2 = (f32[512,8,128]{2,1,0:T(8,128)S(1)}, f32[512,8,128]{2,1,0:T(8,128)}, u32[]{:S(2)}) copy-start(f32[512,8,128]{2,1,0:T(8,128)} %copy-done.1) | copy-start | bytes 6291460
  294.5 4.9 %copy-start.7 = (f32[512,1024]{1,0:T(8,128)S(1)}, f32[512,1024]{1,0:T(8,128)}, u32[]{:S(2)}) copy-start(f32[512,1024]{1,0:T(8,128)} %get-tuple-element.9) | copy-start | bytes 6291460
  294.5 10.9 %slice-start = ((s8[5242880]{0:T(1024)(128)(4,1)}), s8[1048576]{0:T(1024)(128)(4,1)S(1)}, s32[]{:S(2)}) async-start(s8[5242880]{0:T(1024)(128)(4,1)} %bitcast.42), calls=%async_computation.4 | async-start | bytes 2097152
  299.5 6.0 %slice-start.1 = ((s8[5242880]{0:T(1024)(128)(4,1)}), s8[4194304]{0:T(1024)(128)(4,1)S(1)}, s32[]{:S(2)}) async-start(s8[5242880]{0:T(1024)(128)(4,1)} %bitcast.42), calls=%async_computation.5 | async-start | bytes 8388608
  305.4 10.2 %copy-start.5 = (f32[1024]{0:T(1024)}, f32[1024]{0:T(1024)S(1)}, u32[]{:S(2)}) copy-start(f32[1024]{0:T(1024)S(1)} %get-tuple-element.10) | copy-start | bytes 12292
  305.4 10.2 %slice-start.4 = ((s8[5242880]{0:T(1024)(128)(4,1)}), s8[4194304]{0:T(1024)(128)(4,1)S(1)}, s32[]{:S(2)}) async-start(s8[5242880]{0:T(1024)(128)(4,1)} %bitcast.47), calls=%async_computation.8 | async-start | bytes 8388608
  308.5 7.2 %slice-start.5 = ((s8[5242880]{0:T(1024)(128)(4,1)}), s8[1048576]{0:T(1024)(128)(4,1)S(1)}, s32[]{:S(2)}) async-start(s8[5242880]{0:T(1024)(128)(4,1)} %bitcast.47), calls=%async_computation.9 | async-start | bytes 2097152
Sparse Core Ops, SparseCore 0:
  21.8 76.3 all-gather.3
  121.8 172.6 all-reduce.2
where the time goes:
time: 403 us; the launch traced here: 402 us
  waiting for transfers between devices  197 us (49%)
  blocking collectives  128 us (32%)
  matrix products  30.3 us (8%)
  between operations  16.7 us (4%)
  other arithmetic  14.6 us (4%)
  local copies, waits for them, and re-layouts  12 us (3%)
  starting transfers between devices  4.05 us (1%)
    psum x1, waiting for transfers between devices, shards(): summed = lax.psum(partial_sum, 'latent')  168 us
    psum x1, blocking collectives, shards(): grad_dec, loss_sum = lax.psum((bias_term, loss_term), ('expert', 'latent'))  75.9 us
    all_gather x1, blocking collectives, shards(): lax.all_gather(got_lists[None], 'latent', axis=0, tiled=True)  40.8 us
    all_gather x1, waiting for transfers between devices, shards(): lax.all_gather(got_rows[None], 'latent', axis=0, tiled=True)  24 us
    all_to_all x1, blocking collectives, shards(): lax.all_to_all(send_rows, 'expert', split_axis=0, concat_axis=0, tiled=True)  11.2 us
    dot_general x1, matrix products, shards(): jnp.dot(shifted, weights_here, preferred_element_type=jnp.float32)  8.73 us
  transfers between devices with their start and end apart: 3, of which 3 were waited for; matrix products, arithmetic and copies ran while one was open for 2% of the time, Pallas kernels for 0%

commit v1 on v0

--- a/solution.py
+++ b/solution.py
@@ -71,7 +71,7 @@
     )
     bias_term = jnp.sum(error_share, axis=0) - pulled
     loss_term = 0.5 * jnp.sum(error_share * error_share)
-    grad_dec, loss_sum = lax.psum((bias_term, loss_term), ("expert", "latent"))
+    grad_dec, loss_sum = lax.psum(lax.psum((bias_term, loss_term), "latent"), "expert")
     loss = loss_sum / (tokens.shape[0] * n_expert * n_latent)
     return (grad_here.astype(jnp.bfloat16)[None], grad_bias[None], grad_dec, loss)
 

time: 403 us -> 490 us (1.22)
  blocking collectives: 128 us -> 214 us
    psum x1 -> x2, blocking collectives: 75.9 us -> 162 us  [the longest x1 113 us: shards(): lax.psum((bias_term, loss_term), 'latent')]
  transfers between devices with their start and end apart: 3 -> 3, of which waited for: 3 -> 3; matrix products, arithmetic and copies ran while one was open for 2% -> 1% of each run, Pallas kernels for 0% -> 0%
where the time goes in v1:
time: 490 us; the launch traced here: 489 us
  blocking collectives  214 us (44%)
  waiting for transfers between devices  197 us (40%)
  matrix products  30.3 us (6%)
  between operations  16.7 us (3%)
  other arithmetic  14.6 us (3%)
  local copies, waits for them, and re-layouts  12 us (2%)
    psum x1, waiting for transfers between devices, shards(): summed = lax.psum(partial_sum, 'latent')  168 us
    psum x1, blocking collectives, shards(): lax.psum((bias_term, loss_term), 'latent')  113 us
    psum x1, blocking collectives, shards(): lax.psum(lax.psum((bias_term, loss_term), 'latent'), 'expert')  49.1 us
    all_gather x1, blocking collectives, shards(): lax.all_gather(got_lists[None], 'latent', axis=0, tiled=True)  40.8 us
    all_gather x1, waiting for transfers between devices, shards(): lax.all_gather(got_rows[None], 'latent', axis=0, tiled=True)  24 us
    all_to_all x1, blocking collectives, shards(): lax.all_to_all(send_rows, 'expert', split_axis=0, concat_axis=0, tiled=True)  11.2 us
  transfers between devices with their start and end apart: 3, of which 3 were waited for; matrix products, arithmetic and copies ran while one was open for 1% of the time, Pallas kernels for 0%

profile of v1, /device:TPU:1, one launch (start us, length us, event | category | flops | bytes accessed | tf_op | source)
XLA Modules:
  0.0 488.5 jit_solution(2492645457196000848)
XLA Ops:
  7.2 0.0 all-gather.4.cloned.1.call-start
  7.2 0.7 fusion.24
  8.0 0.8 select_reduce_fusion
  8.8 0.7 fusion.25
  9.5 0.9 scatter_custom_fusion
  10.4 11.2 %all_to_all.10 = bf16[8,2,2560]{2,1,0:T(2,128)(2,1)} all-to-all(bf16[8,2,2560]{2,1,0:T(2,128)(2,1)S(1)} %reshape.33), channel_id=1, replica_groups=mesh['expert'=8,'latent'=32] {'expert'}, dimensions={0} | all-to-all | bytes 163840 | tf_op jit(solution)/shard_map/all_to_all | solution.py:26
  21.6 0.0 all-gather.4.cloned.1.call-update
  21.7 0.8 scatter_custom_fusion.1
  22.4 0.7 reshape.68
  23.1 4.0 all-to-all-start.1
  27.1 4.5 all-to-all-done.1
  31.6 0.5 broadcast.43
  32.2 0.7 reduce.4
  32.8 0.1 reshape.69
  32.9 40.8 %all-gather.1 = s32[256,2,64]{2,1,0:T(2,128)S(1)} all-gather(s32[8,2,64]{2,1,0:T(2,128)S(1)} %reshape.69), channel_id=3, replica_groups=mesh['expert'=8,'latent'=32] {'latent'}, dimensions={0}, use_global_device_ids=true | all-gather | bytes 135168 | tf_op jit(solution)/shard_map/all_gather | solution.py:31
  73.7 0.1 copy.12
  73.8 0.2 compare_reduce_fusion
  74.1 0.1 copy.13
  74.2 24.0 %all-gather.4.cloned.1.call-done = bf16[256,2,2560]{2,1,0:T(2,128)(2,1)} async-done(((bf16[8,2,2560]{2,1,0:T(2,128)(2,1)}), bf16[256,2,2560]{2,1,0:T(2,128)(2,1)}) %all-gather.4.cloned.1.call-update) | async-done | bytes 2621456 | tf_op jit(solution)/shard_map/all_gather | solution.py:30
  98.1 3.5 convert_element_type.56
  101.7 2.3 subtract_convert_fusion
  104.0 0.0 copy-start.6
  104.0 2.6 convert_element_type.47
  106.6 0.6 broadcast_in_dim.32
  107.2 0.0 copy-start.1
  107.2 0.0 copy-done.6
  107.2 0.0 slice-start.3
  107.3 8.7 %fusion.11 = (bf16[512,1024]{1,0:T(8,128)(2,1)S(1)}, f32[512,1024]{1,0:T(8,128)}) fusion(f32[64,8,8,128]{3,2,1,0:T(8,128)S(1)} %bitcast.51, f32[1024]{0:T(1024)S(1)} %bitcast.57, bf16[512,2560]{1,0:T(8,128)(2,1)} %convert_element_type.47, bf16[1,2560,1024]{2,1,0:T(8,128)(2,1)} %param.9), kind=kOutput, calls=%fused_computation.19 | convolution fusion | flops 2686451712 | bytes 13111296 | tf_op jit(solution)/shard_map/dot_general | solution.py:45
  116.0 1.0 copy-done.3
  117.0 4.7 fusion.4
  121.7 0.0 all-reduce.4.cloned.1.call-update
  121.7 0.1 convert_reduce_fusion
  121.8 1.6 copy-done
  123.4 2.9 reshape.36
  126.4 168.2 %all-reduce.4.cloned.1.call-done = f32[512,2560]{1,0:T(8,128)} async-done(((f32[512,2560]{1,0:T(8,128)}), f32[512,2560]{1,0:T(8,128)}) %all-reduce.4.cloned.1.call-update) | async-done | bytes 5242896 | tf_op jit(solution)/shard_map/psum | solution.py:54
  294.5 4.9 %subtract_multiply_fusion = f32[512,2560]{1,0:T(8,128)S(1)} fusion(f32[512,2560]{1,0:T(8,128)} %reshape.36, f32[512,2560]{1,0:T(8,128)} %all-reduce.4.cloned.1.call-done, f32[512]{0:T(512)S(1)} %convert_reduce_fusion, f32[2560]{0:T(1024)S(1)} %copy-done.4), kind=kLoop, calls=%fused_computation.11 | loop fusion | flops 3932160 | bytes 15740928 | tf_op jit(solution)/shard_map/mul | solution.py:55
  299.5 0.0 slice-start.1
  299.5 5.9 %fusion.26 = (f32[1024]{0:T(1024)S(1)}, bf16[512,1024]{1,0:T(8,128)(2,1)S(1)}) fusion(f32[64,8,8,128]{3,2,1,0:T(8,128)S(1)} %bitcast.52, bf16[1,2560,1024]{2,1,0:T(8,128)(2,1)} %param.9, f32[512,2560]{1,0:T(8,128)S(1)} %subtract_multiply_fusion, f32[512,1024]{1,0:T(8,128)S(1)} %copy-done.7, f32[1024]{0:T(1024)S(1)} %bitcast.58), kind=kOutput, calls=%fused_computation.40 | convolution fusion | flops 2688809984 | bytes 15736832 | tf_op jit(solution)/shard_map/dot_general | solution.py:58
  305.4 0.0 copy-start.5
  305.4 0.0 slice-done
  305.4 0.0 slice-start.4
  305.5 3.0 fusion.9
  308.5 0.0 slice-start.5
  308.5 6.5 %fusion.8 = bf16[1,2560,1024]{2,1,0:T(8,128)(2,1)} fusion(f32[2560,1024]{1,0:T(8,128)S(1)} %fusion.9, bf16[512,1024]{1,0:T(8,128)(2,1)} %copy-done.3, f32[512,2560]{1,0:T(8,128)S(1)} %subtract_multiply_fusion), kind=kOutput, calls=%fused_computation.14 | convolution fusion | flops 2690908160 | bytes 22020096 | tf_op jit(solution)/shard_map/dot_general | solution.py:65
  315.0 0.6 multiply_reduce_fusion
  315.6 1.5 fusion.16
  317.8 113.0 %all-reduce = (f32[2560]{0:T(1024)S(1)}, f32[]{:T(128)}) all-reduce(f32[2560]{0:T(1024)S(1)} %sub.28, f32[]{:T(128)S(6)} %mul_shard_map.3), channel_id=1, replica_groups=mesh['expert'=8,'latent'=32] {'latent'}, use_global_device_ids=true, to_apply=%region_8.9 | all-reduce | flops 2561 | bytes 20488 | tf_op jit(solution)/shard_map/psum | solution.py:74
  430.8 49.1 %all-reduce.1 = (f32[2560]{0:T(1024)}, f32[]{:T(128)}) all-reduce(f32[2560]{0:T(1024)S(1)} %get-tuple-element.6, f32[]{:T(128)} %get-tuple-element.7), channel_id=1, replica_groups=mesh['expert'=8,'latent'=32] {'expert'}, use_global_device_ids=true, to_apply=%region_9.10 | all-reduce | flops 2561 | bytes 20488 | tf_op jit(solution)/shard_map/psum | solution.py:74
  (28 shorter events, 0.1 us)
Async XLA Ops:
  7.2 94.5 %copy-start.4 = (f32[2560]{0:T(1024)S(1)}, f32[2560]{0:T(1024)}, u32[]{:S(2)}) copy-start(f32[2560]{0:T(1024)} %param.11) | copy-start | bytes 30724
  7.2 91.0 %all-gather.4.cloned.1.call-start = ((), (), s32[]{:S(2)}) async-start(), calls=%async_computation.3 | async-start | bytes 2703360 | tf_op jit(solution)/shard_map/all_gather | solution.py:30
  23.1 8.5 %all-to-all-start.1 = ((s32[8,1,128]{2,1,0:T(1,128)}), s32[8,1,128]{2,1,0:T(1,128)S(1)}, u32[]{:S(2)}, u32[]{:S(2)}) async-start(s32[8,1,128]{2,1,0:T(1,128)} %reshape.68), calls=%async_computation.1 | async-start | bytes 8192 | tf_op jit(solution)/shard_map/all_to_all | solution.py:27
  27.1 267.4 %all-reduce.4.cloned.1.call-start = ((), (), s32[]{:S(2)}) async-start(), calls=%async_computation.2 | async-start | bytes 10485760 | tf_op jit(solution)/shard_map/psum | solution.py:54
  104.0 3.2 copy-start.6
  106.6 10.4 %slice-start.2 = ((s8[5242880]{0:T(1024)(128)(4,1)}), s8[4194304]{0:T(1024)(128)(4,1)S(1)}, s32[]{:S(2)}) async-start(s8[5242880]{0:T(1024)(128)(4,1)} %bitcast.45), calls=%async_computation.6 | async-start | bytes 8388608
  107.2 8.8 %copy-start.1 = (f32[512,8,128]{2,1,0:T(8,128)}, f32[512,8,128]{2,1,0:T(8,128)S(1)}, u32[]{:S(2)}) copy-start(f32[512,8,128]{2,1,0:T(8,128)S(1)} %broadcast_in_dim.32) | copy-start | bytes 6291460
  107.2 9.7 %slice-start.3 = ((s8[5242880]{0:T(1024)(128)(4,1)}), s8[1048576]{0:T(1024)(128)(4,1)S(1)}, s32[]{:S(2)}) async-start(s8[5242880]{0:T(1024)(128)(4,1)} %bitcast.45), calls=%async_computation.7 | async-start | bytes 2097152
  116.0 1.0 copy-start.3
  121.7 1.7 copy-start
  126.3 173.1 %copy-start.2 = (f32[512,8,128]{2,1,0:T(8,128)S(1)}, f32[512,8,128]{2,1,0:T(8,128)}, u32[]{:S(2)}) copy-start(f32[512,8,128]{2,1,0:T(8,128)} %copy-done.1) | copy-start | bytes 6291460
  294.5 4.9 %copy-start.7 = (f32[512,1024]{1,0:T(8,128)S(1)}, f32[512,1024]{1,0:T(8,128)}, u32[]{:S(2)}) copy-start(f32[512,1024]{1,0:T(8,128)} %get-tuple-element.11) | copy-start | bytes 6291460
  294.5 10.9 %slice-start = ((s8[5242880]{0:T(1024)(128)(4,1)}), s8[1048576]{0:T(1024)(128)(4,1)S(1)}, s32[]{:S(2)}) async-start(s8[5242880]{0:T(1024)(128)(4,1)} %bitcast.42), calls=%async_computation.4 | async-start | bytes 2097152
  299.5 6.0 %slice-start.1 = ((s8[5242880]{0:T(1024)(128)(4,1)}), s8[4194304]{0:T(1024)(128)(4,1)S(1)}, s32[]{:S(2)}) async-start(s8[5242880]{0:T(1024)(128)(4,1)} %bitcast.42), calls=%async_computation.5 | async-start | bytes 8388608
  305.4 10.2 %copy-start.5 = (f32[1024]{0:T(1024)}, f32[1024]{0:T(1024)S(1)}, u32[]{:S(2)}) copy-start(f32[1024]{0:T(1024)S(1)} %get-tuple-element.12) | copy-start | bytes 12292
  305.4 10.2 %slice-start.4 = ((s8[5242880]{0:T(1024)(128)(4,1)}), s8[4194304]{0:T(1024)(128)(4,1)S(1)}, s32[]{:S(2)}) async-start(s8[5242880]{0:T(1024)(128)(4,1)} %bitcast.47), calls=%async_computation.8 | async-start | bytes 8388608
  308.5 7.2 %slice-start.5 = ((s8[5242880]{0:T(1024)(128)(4,1)}), s8[1048576]{0:T(1024)(128)(4,1)S(1)}, s32[]{:S(2)}) async-start(s8[5242880]{0:T(1024)(128)(4,1)} %bitcast.47), calls=%async_computation.9 | async-start | bytes 2097152
Sparse Core Ops, SparseCore 0:
  21.8 76.3 all-gather.3
  121.8 172.6 all-reduce.3
